TPU v7x, 32 devices: a whole 2x2x4 slice. The times are simulated.
32 devices in a mesh: tm: 8 (over z, x), space: 4 (over y, core).
Axes of the slice: x: 2, y: 2, z: 4, core: 2. Of those that a mesh axis runs over, the one named last changes fastest.
Arguments:
- queries: bfloat16 [8, 512, 2048], P('tm', 'space'), may hold values from -180 to 180
- key_vectors: bfloat16 [8, 512, 2048], P('tm', 'space'), may hold values from -6 to 6
- value_vectors: bfloat16 [8, 512, 2048], P('tm', 'space'), may hold values from -96 to 96
- block_lists: int32 [4, 3], replicated, may hold values from 0 to 3, as said below
- step_sizes: float32 [8, 512, 16], P(None, ('space', 'tm')), may hold values from 0.004 to 0.6, as said below
- decay_rates: float32 [16], replicated, may hold values from 0.7 to 1.4
- skip_gains: float32 [16], replicated, may hold values from 0.5 to 1.5
- pre_gain: float32 [2048], replicated, may hold values from 0.25 to 1.75
- state_in_weight: bfloat16 [2048, 64], replicated, may hold values from -0.125 to 0.125
- state_out_weight: bfloat16 [2048, 64], replicated, may hold values from -0.125 to 0.125
- post_gain: float32 [2048], replicated, may hold values from 0.25 to 1.75
Outputs:
- mixed_out: bfloat16 [8, 512, 2048], P('tm', 'space')
Inputs may be any that keep to these rules, and one draw needn't show every extreme that they name: `block_lists`: row i lists 3 different key blocks; its first entry is i itself. `step_sizes`: positive step sizes.
All inputs are finite; a program needn't handle non-finite values.
Results may differ from a plain program's by a relative error of at most 0.01.
Values may be sent and summed in bfloat16 or wider, within the bound.
A program may use at most 64 MiB of HBM per device.

v0:
```python
import math
import jax
import jax.numpy as jnp
from jax import lax
from jax.sharding import PartitionSpec as P

SHARED_HEADS = 16
HEAD_DIM = 128
BLOCK = 128


def rms_scale(values, gain_row):
    return values * lax.rsqrt(jnp.mean(values * values, axis=-1, keepdims=True) + 1e-05) * gain_row


def attend_heads(stacked, block_lists):
    query_rows, key_rows, value_rows = stacked
    total_rows, head_count, head_width = query_rows.shape
    block_count = total_rows // BLOCK
    group_size = math.gcd(block_count, max(1, 512 // BLOCK))
    list_width = block_lists.shape[1]
    score_scale = 1.0 / math.sqrt(head_width)
    query_blocks = query_rows.reshape(block_count, BLOCK, head_count, head_width)
    key_blocks = key_rows.reshape(block_count, BLOCK, head_count, head_width)
    value_blocks = value_rows.reshape(block_count, BLOCK, head_count, head_width)

    def attend_group(group_index):
        first_block = group_index * group_size
        chosen = lax.dynamic_slice_in_dim(block_lists, first_block, group_size, 0)
        query_group = lax.dynamic_slice_in_dim(query_blocks, first_block, group_size, 0)
        key_group = jnp.take(key_blocks, chosen, axis=0).reshape(
            group_size, list_width * BLOCK, head_count, head_width
        )
        value_group = jnp.take(value_blocks, chosen, axis=0).reshape(
            group_size, list_width * BLOCK, head_count, head_width
        )
        scores = (
            jnp.einsum(
                "gqhd,gkhd->ghqk", query_group, key_group, preferred_element_type=jnp.float32
            )
            * score_scale
        )
        row_max = jnp.max(scores, axis=-1, keepdims=True)
        exp_scores = jnp.exp(scores - row_max)
        totals = jnp.sum(exp_scores, axis=-1)
        weights_bf = exp_scores.astype(jnp.bfloat16)
        summed = jnp.einsum(
            "ghqk,gkhd->gqhd", weights_bf, value_group, preferred_element_type=jnp.float32
        )
        return (summed / jnp.transpose(totals, (0, 2, 1))[..., None]).astype(jnp.bfloat16)

    attended = lax.map(attend_group, jnp.arange(block_count // group_size, dtype=jnp.int32))
    return attended.reshape(total_rows, head_count, head_width)


def attend_grouped(stacked, block_lists):
    query_rows, key_rows, value_rows = stacked
    total_rows = query_rows.shape[0]
    head_count = query_rows.shape[2]
    head_width = query_rows.shape[3]
    flat = tuple(
        (
            piece.reshape(total_rows, head_count, head_width)
            for piece in (query_rows, key_rows, value_rows)
        )
    )
    result = attend_heads(flat, block_lists)
    return result.reshape(total_rows, 1, head_count, head_width)


def temporal_mix(
    normed, step_block, decay_rates, skip_gains, state_in_weight, state_out_weight, post_gain
):
    frame_count, token_count, channel_count = normed.shape
    head_count = step_block.shape[2]
    head_width = channel_count // head_count
    flat_rows = normed.reshape(frame_count * token_count, channel_count)
    b_in = jnp.dot(flat_rows, state_in_weight, preferred_element_type=jnp.float32).reshape(
        frame_count, token_count, -1
    )
    c_out = jnp.dot(flat_rows, state_out_weight, preferred_element_type=jnp.float32).reshape(
        frame_count, token_count, -1
    )
    gram_matrix = jnp.einsum("tkn,skn->kts", c_out, b_in, precision=lax.Precision.HIGHEST)
    log_decay = -step_block * decay_rates
    frame_index = jnp.arange(frame_count, dtype=jnp.int32)
    between = (
        (frame_index[None, :, None] < frame_index[None, None, :])
        & (frame_index[None, None, :] <= frame_index[:, None, None])
    ).astype(jnp.float32)
    seg_sum = jnp.einsum("tsr,rkh->ktsh", between, log_decay, precision=lax.Precision.HIGHEST)
    causal = frame_index[None, :] <= frame_index[:, None]
    decay_matrix = jnp.where(causal[None, :, :, None], jnp.exp(seg_sum), jnp.zeros_like(seg_sum))
    weight_matrix = (
        gram_matrix[..., None] * decay_matrix * jnp.transpose(step_block, (1, 0, 2))[:, None, :, :]
    )
    x_values = normed.astype(jnp.float32).reshape(frame_count, token_count, head_count, head_width)
    y_mixed = (
        jnp.einsum("ktsh,skhp->tkhp", weight_matrix, x_values, precision=lax.Precision.HIGHEST)
        + skip_gains[:, None] * x_values
    )
    y_flat = y_mixed.reshape(frame_count, token_count, channel_count)
    return rms_scale(y_flat, post_gain).astype(jnp.bfloat16)


def body(
    queries,
    key_vectors,
    value_vectors,
    block_lists,
    step_sizes,
    decay_rates,
    skip_gains,
    pre_gain,
    state_in_weight,
    state_out_weight,
    post_gain,
):
    token_count = queries.shape[1]
    channel_count = queries.shape[2]
    query_rows = queries.reshape(token_count, SHARED_HEADS, HEAD_DIM)
    key_rows = key_vectors.reshape(token_count, SHARED_HEADS, HEAD_DIM)
    value_rows = value_vectors.reshape(token_count, SHARED_HEADS, HEAD_DIM)
    by_token = None
    attended = None
    space_count = lax.axis_size("space")
    local_heads = SHARED_HEADS // space_count
    query_split = query_rows.reshape(token_count, space_count, local_heads, HEAD_DIM)
    key_split = key_rows.reshape(token_count, space_count, local_heads, HEAD_DIM)
    value_split = value_rows.reshape(token_count, space_count, local_heads, HEAD_DIM)
    received = attend_grouped(
        (
            lax.all_to_all(query_split, "space", split_axis=1, concat_axis=0, tiled=True),
            lax.all_to_all(key_split, "space", split_axis=1, concat_axis=0, tiled=True),
            lax.all_to_all(value_split, "space", split_axis=1, concat_axis=0, tiled=True),
        ),
        block_lists=block_lists,
    )
    gathered = received.reshape(received.shape[0], local_heads, HEAD_DIM)
    attended = lax.all_to_all(gathered, "space", split_axis=0, concat_axis=1, tiled=True)
    normed = rms_scale(
        attended.reshape(1, token_count, channel_count).astype(jnp.float32), pre_gain
    ).astype(jnp.bfloat16)
    by_token = lax.all_to_all(normed, "tm", split_axis=1, concat_axis=0, tiled=True)
    mixed_tokens = temporal_mix(
        by_token, step_sizes, decay_rates, skip_gains, state_in_weight, state_out_weight, post_gain
    )
    return lax.all_to_all(mixed_tokens, "tm", split_axis=0, concat_axis=1, tiled=True)


def solution(mesh):
    placed = (
        P("tm", "space", None),
        P("tm", "space", None),
        P("tm", "space", None),
        P(),
        P(None, ("space", "tm"), None),
        P(),
        P(),
        P(),
        P(),
        P(),
        P(),
    )
    return jax.shard_map(
        body, mesh=mesh, in_specs=placed, out_specs=P("tm", "space", None), check_vma=False
    )
```

profile of v0, /device:TPU:0, one launch (start us, length us, event | category | flops | bytes accessed | tf_op | source)
XLA Modules:
  0.0 110.1 jit_solution(432417027500597041)
XLA Ops:
  0.0 1.4 %copy.111 = bf16[1,128,2048]{1,2,0:T(8,128)(2,1)S(1)} copy(bf16[1,128,2048]{2,1,0:T(8,128)(2,1)} %param.14) | data formatting | bytes 1048576 | tf_op args[1]
  1.4 1.1 copy.112
  2.5 4.2 %all-to-all-start.1 = ((bf16[128,4,4,128]{3,2,0,1:T(4,128)(2,1)}), bf16[128,4,4,128]{3,2,0,1:T(4,128)(2,1)S(1)}, u32[]{:S(2)}, u32[]{:S(2)}) async-start(bf16[128,4,4,128]{3,2,0,1:T(4,128)(2,1)} %copy.112), calls=%async_computation.1 | async-start | bytes 1048576 | tf_op jit(solution)/shard_map/all_to_all | solution.py:134
  6.7 0.3 copy.108
  7.0 1.1 copy.109
  8.1 7.5 %all-to-all-done.1 = bf16[128,4,4,128]{3,2,0,1:T(4,128)(2,1)S(1)} async-done(((bf16[128,4,4,128]{3,2,0,1:T(4,128)(2,1)}), bf16[128,4,4,128]{3,2,0,1:T(4,128)(2,1)S(1)}, u32[]{:S(2)}, u32[]{:S(2)}) %all-to-all-start.1) | async-done | bytes 524320 | tf_op jit(solution)/shard_map/all_to_all | solution.py:134
  15.5 3.5 %all-to-all-start = ((bf16[128,4,4,128]{3,2,0,1:T(4,128)(2,1)}), bf16[128,4,4,128]{3,2,0,1:T(4,128)(2,1)S(1)}, u32[]{:S(2)}, u32[]{:S(2)}) async-start(bf16[128,4,4,128]{3,2,0,1:T(4,128)(2,1)} %copy.109), calls=%async_computation | async-start | bytes 1048576 | tf_op jit(solution)/shard_map/all_to_all | solution.py:135
  19.1 0.3 copy.114
  19.4 1.0 copy.115
  20.4 1.9 %gather_fusion.1 = bf16[12,128,4,128]{3,2,1,0:T(4,128)(2,1)S(1)} fusion(bf16[4,128,4,128]{3,2,1,0:T(4,128)(2,1)S(1)} %bitcast.92, s32[1024]{0:T(1024)S(1)} %pad_clamp_fusion), kind=kCustom, calls=%fused_computation.1.clone | custom fusion | bytes 3145776 | tf_op jit(solution)/shard_map/while/body/eval_jaxpr/jit(_take)/gather | solution.py:31
  22.4 5.5 %all-to-all-done = bf16[128,4,4,128]{3,2,0,1:T(4,128)(2,1)S(1)} async-done(((bf16[128,4,4,128]{3,2,0,1:T(4,128)(2,1)}), bf16[128,4,4,128]{3,2,0,1:T(4,128)(2,1)S(1)}, u32[]{:S(2)}, u32[]{:S(2)}) %all-to-all-start) | async-done | bytes 524320 | tf_op jit(solution)/shard_map/all_to_all | solution.py:135
  27.8 3.5 %all-to-all-start.2 = ((bf16[128,4,4,128]{3,0,2,1:T(8,128)(2,1)}), bf16[128,4,4,128]{3,0,2,1:T(8,128)(2,1)S(1)}, u32[]{:S(2)}, u32[]{:S(2)}) async-start(bf16[128,4,4,128]{3,0,2,1:T(8,128)(2,1)} %copy.115), calls=%async_computation.2 | async-start | bytes 1048576 | tf_op jit(solution)/shard_map/all_to_all | solution.py:133
  31.3 3.2 %gather_fusion = bf16[12,128,4,128]{3,2,1,0:T(4,128)(2,1)} fusion(bf16[4,128,4,128]{3,2,1,0:T(4,128)(2,1)S(1)} %bitcast.93, s32[1024]{0:T(1024)S(1)} %pad_clamp_fusion), kind=kCustom, calls=%fused_computation.clone | custom fusion | bytes 3145776 | tf_op jit(solution)/shard_map/while/body/eval_jaxpr/jit(_take)/gather | solution.py:34
  34.5 2.8 %broadcast_select_fusion = (bf16[4,3,128,4,128]{4,3,2,1,0:T(4,128)(2,1)S(1)}, bf16[4,3,128,4,128]{4,3,2,1,0:T(4,128)(2,1)S(1)}) fusion(bf16[4,3,128,4,128]{4,3,2,1,0:T(4,128)(2,1)S(1)} %bitcast.95, pred[4,3]{1,0:T(4,128)(4,1)S(1)} %compare_and_fusion, bf16[4,3,128,4,128]{4,3,2,1,0:T(4,128)(2,1)} %bitcast.96), kind=kLoop, calls=%fused_computation.10 | loop fusion | flops 1572864 | bytes 6291468 | tf_op jit(solution)/shard_map/while/body/eval_jaxpr/jit(_take)/select_n | solution.py:31
  37.3 1.6 %copy.110 = bf16[4,3,128,4,128]{4,2,1,3,0:T(8,128)(2,1)} copy(bf16[4,3,128,4,128]{4,3,2,1,0:T(4,128)(2,1)S(1)} %get-tuple-element.17) | data formatting | bytes 3145728 | tf_op jit(solution)/shard_map/while/body/eval_jaxpr/jit(_take)/select_n | solution.py:34
  38.9 0.4 copy.113
  39.3 0.9 all-to-all-done.2
  40.1 0.6 bitcast_reduce_fusion
  40.7 0.5 fusion.1
  41.3 0.9 copy-done.1
  42.1 1.0 fusion.18
  43.2 0.4 copy.118
  43.6 11.2 %all_to_all.75 = bf16[512,4,128]{2,1,0:T(4,128)(2,1)S(1)} all-to-all(bf16[512,4,128]{2,1,0:T(4,128)(2,1)S(1)} %copy.118), channel_id=1, replica_groups=mesh['tm'=8,'space'=4] {'space'}, dimensions={0} | all-to-all | bytes 1048576 | tf_op jit(solution)/shard_map/all_to_all | solution.py:140
  54.9 0.3 copy.120
  55.2 0.2 multiply_reduce_fusion.1
  55.6 0.3 multiply_convert_fusion.1
  55.9 0.9 copy.121
  56.9 0.5 broadcast.154
  57.4 3.7 %reduce.7 = bf16[128,2048]{1,0:T(8,128)(2,1)S(1)} reduce(bf16[128,1,2048]{2,1,0:T(2,128)(2,1)S(1)} %bitcast.100, bf16[]{:T(256)} %broadcast.154), dimensions={1}, to_apply=%bitcast.81.reduce_sub_computation | reduce | bytes 1048578
  61.2 1.2 %reshape.227 = bf16[8,2,16384]{2,1,0:T(2,128)(2,1)} reshape(bf16[128,2048]{1,0:T(8,128)(2,1)S(1)} %reduce.7) | data formatting | bytes 1048576
  62.3 6.5 %all-to-all-start.4 = ((bf16[8,2,16384]{2,1,0:T(2,128)(2,1)}), bf16[8,2,16384]{2,1,0:T(2,128)(2,1)S(1)}, u32[]{:S(2)}, u32[]{:S(2)}) async-start(bf16[8,2,16384]{2,1,0:T(2,128)(2,1)} %reshape.227), calls=%async_computation.4 | async-start | bytes 1048576 | tf_op jit(solution)/shard_map/all_to_all | solution.py:144
  68.9 14.1 %all-to-all-done.4 = bf16[8,2,16384]{2,1,0:T(2,128)(2,1)S(1)} async-done(((bf16[8,2,16384]{2,1,0:T(2,128)(2,1)}), bf16[8,2,16384]{2,1,0:T(2,128)(2,1)S(1)}, u32[]{:S(2)}, u32[]{:S(2)}) %all-to-all-start.4) | async-done | bytes 524320 | tf_op jit(solution)/shard_map/all_to_all | solution.py:144
  82.9 0.5 reshape.228
  83.5 3.0 %bitcast_reduce_fusion.2 = bf16[128,2048]{1,0:T(8,128)(2,1)S(1)} fusion(bf16[128,1,2048]{2,1,0:T(2,128)(2,1)S(1)} %reshape.228), kind=kLoop, calls=%fused_computation.52 | loop fusion | bytes 1048576 | tf_op jit(solution)/shard_map/all_to_all | solution.py:144
  86.6 0.3 copy.135
  86.9 0.3 fusion.24
  87.2 0.2 copy-done.4
  87.4 0.3 fusion.26
  87.7 0.3 fusion.29
  88.0 0.4 fusion.14
  88.4 0.4 copy.127
  88.9 1.4 %multiply_reduce_fusion = (f32[8,16]{0,1:T(8,128)S(1)}, f32[8,16,16,128]{3,0,2,1:T(8,128)S(1)}) fusion(bf16[8,16,16,128]{3,2,1,0:T(8,128)(2,1)S(1)} %bitcast.108, f32[16]{0:T(128)S(1)} %copy-done.10, f32[16,8,8,16]{2,1,3,0:T(8,128)S(1)} %copy.127), kind=kOutput, calls=%fused_computation.23 | convolution fusion | flops 26476416 | bytes 1638976 | tf_op jit(solution)/shard_map/ktsh,skhp->tkhp/dot_general | solution.py:99
  90.3 0.2 copy.129
  90.5 0.2 reshape.191
  90.8 0.4 copy-done.7
  91.2 0.2 multiply_convert_fusion
  91.4 17.9 %all_to_all.76 = bf16[8,16,2048]{2,1,0:T(8,128)(2,1)S(1)} all-to-all(bf16[8,16,2048]{2,1,0:T(8,128)(2,1)S(1)} %multiply_convert_fusion), channel_id=1, replica_groups=mesh['tm'=8,'space'=4] {'tm'}, dimensions={0} | all-to-all | bytes 1048576 | tf_op jit(solution)/shard_map/all_to_all | solution.py:148
  109.3 0.8 copy.151
  (33 shorter events, 0.6 us)
Async XLA Ops:
  0.0 86.9 %copy-start = (bf16[2048,64]{0,1:T(8,128)(2,1)S(1)}, bf16[2048,64]{0,1:T(8,128)(2,1)}, u32[]{:S(2)}) copy-start(bf16[2048,64]{0,1:T(8,128)(2,1)} %param.21) | copy-start | bytes 786436
  0.0 6.7 %copy-start.2 = (bf16[1,128,2048]{2,1,0:T(8,128)(2,1)S(1)}, bf16[1,128,2048]{2,1,0:T(8,128)(2,1)}, u32[]{:S(2)}) copy-start(bf16[1,128,2048]{2,1,0:T(8,128)(2,1)} %param.15) | copy-start | bytes 1572868
  2.5 13.1 %all-to-all-start.1 = ((bf16[128,4,4,128]{3,2,0,1:T(4,128)(2,1)}), bf16[128,4,4,128]{3,2,0,1:T(4,128)(2,1)S(1)}, u32[]{:S(2)}, u32[]{:S(2)}) async-start(bf16[128,4,4,128]{3,2,0,1:T(4,128)(2,1)} %copy.112), calls=%async_computation.1 | async-start | bytes 1048576 | tf_op jit(solution)/shard_map/all_to_all | solution.py:134
  6.7 12.3 %copy-start.8 = (s32[4,3]{1,0:T(4,128)S(1)}, s32[4,3]{1,0:T(4,128)}, u32[]{:S(2)}) copy-start(s32[4,3]{1,0:T(4,128)} %param.16) | copy-start | bytes 148
  6.7 12.4 %copy-start.3 = (bf16[1,128,2048]{2,1,0:T(8,128)(2,1)S(1)}, bf16[1,128,2048]{2,1,0:T(8,128)(2,1)}, u32[]{:S(2)}) copy-start(bf16[1,128,2048]{2,1,0:T(8,128)(2,1)} %param.13) | copy-start | bytes 1572868
  15.5 12.3 %all-to-all-start = ((bf16[128,4,4,128]{3,2,0,1:T(4,128)(2,1)}), bf16[128,4,4,128]{3,2,0,1:T(4,128)(2,1)S(1)}, u32[]{:S(2)}, u32[]{:S(2)}) async-start(bf16[128,4,4,128]{3,2,0,1:T(4,128)(2,1)} %copy.109), calls=%async_computation | async-start | bytes 1048576 | tf_op jit(solution)/shard_map/all_to_all | solution.py:135
  27.8 12.3 %all-to-all-start.2 = ((bf16[128,4,4,128]{3,0,2,1:T(8,128)(2,1)}), bf16[128,4,4,128]{3,0,2,1:T(8,128)(2,1)S(1)}, u32[]{:S(2)}, u32[]{:S(2)}) async-start(bf16[128,4,4,128]{3,0,2,1:T(8,128)(2,1)} %copy.115), calls=%async_computation.2 | async-start | bytes 1048576 | tf_op jit(solution)/shard_map/all_to_all | solution.py:133
  40.7 1.4 %copy-start.1 = (bf16[4,3,128,4,128]{4,2,1,3,0:T(8,128)(2,1)S(1)}, bf16[4,3,128,4,128]{4,2,1,3,0:T(8,128)(2,1)}, u32[]{:S(2)}) copy-start(bf16[4,3,128,4,128]{4,2,1,3,0:T(8,128)(2,1)} %copy.110) | copy-start | bytes 4718596
  54.9 0.7 copy-start.6
  57.4 11.4 %copy-start.5 = (f32[8,16,16]{2,1,0:T(8,128)S(1)}, f32[8,16,16]{2,1,0:T(8,128)}, u32[]{:S(2)}) copy-start(f32[8,16,16]{2,1,0:T(8,128)} %param.17) | copy-start | bytes 24580
  57.4 11.4 %copy-start.9 = (f32[16]{0:T(128)S(1)}, f32[16]{0:T(128)}, u32[]{:S(2)}) copy-start(f32[16]{0:T(128)} %param.18) | copy-start | bytes 196
  62.3 20.6 %all-to-all-start.4 = ((bf16[8,2,16384]{2,1,0:T(2,128)(2,1)}), bf16[8,2,16384]{2,1,0:T(2,128)(2,1)S(1)}, u32[]{:S(2)}, u32[]{:S(2)}) async-start(bf16[8,2,16384]{2,1,0:T(2,128)(2,1)} %reshape.227), calls=%async_computation.4 | async-start | bytes 1048576 | tf_op jit(solution)/shard_map/all_to_all | solution.py:144
  86.5 1.0 copy-start.4
  87.7 1.1 %copy-start.10 = (f32[16]{0:T(128)S(1)}, f32[16]{0:T(128)}, u32[]{:S(2)}) copy-start(f32[16]{0:T(128)} %param.19) | copy-start | bytes 196
  90.5 0.7 copy-start.7
where the time goes:
time: 111 us; the launch traced here: 110 us
  blocking collectives  29.1 us (26%)
  waiting for transfers between devices  27.9 us (25%)
  local copies, waits for them, and re-layouts  22.8 us (21%)
  starting transfers between devices  17.6 us (16%)
  other arithmetic  7.92 us (7%)
  matrix products  4.28 us (4%)
    all_to_all x1, blocking collectives, body(): lax.all_to_all(mixed_tokens, 'tm', split_axis=0, concat_axis=1, tiled=True)  17.9 us
    all_to_all x1, waiting for transfers between devices, body(): lax.all_to_all(normed, 'tm', split_axis=1, concat_axis=0, tiled=True)  14.1 us
    all_to_all x1, blocking collectives, body(): lax.all_to_all(gathered, 'space', split_axis=0, concat_axis=1, tiled=True)  11.2 us
    all_to_all x1, waiting for transfers between devices, body(): lax.all_to_all(key_split, 'space', split_axis=1, concat_axis=0, tiled=True)  7.49 us
    unnamed x31, local copies, waits for them, and re-layouts  7.03 us
    all_to_all x1, starting transfers between devices, body(): lax.all_to_all(normed, 'tm', split_axis=1, concat_axis=0, tiled=True)  6.46 us
    all_to_all x1, waiting for transfers between devices, body(): lax.all_to_all(value_split, 'space', split_axis=1, concat_axis=0, tiled=T...  5.49 us
    all_to_all x1, starting transfers between devices, body(): lax.all_to_all(key_split, 'space', split_axis=1, concat_axis=0, tiled=True)  4.24 us
  transfers between devices with their start and end apart: 4, of which 4 were waited for; matrix products, arithmetic and copies ran while one was open for 11% of the time, Pallas kernels for 0%

commit v1 on v0

--- a/solution.py
+++ b/solution.py
@@ -7,6 +7,29 @@
 SHARED_HEADS = 16
 HEAD_DIM = 128
 BLOCK = 128
+
+
+def in_blocks(array, dim, size):
+    lengths = array.shape
+    blocks = array.reshape(*lengths[:dim], size, lengths[dim] // size, *lengths[dim + 1 :])
+    return jnp.moveaxis(blocks, dim, 0)
+
+
+def in_order(blocks, dim):
+    blocks = jnp.moveaxis(blocks, 0, dim)
+    lengths = blocks.shape
+    return blocks.reshape(*lengths[:dim], lengths[dim] * lengths[dim + 1], *lengths[dim + 2 :])
+
+
+def swapped_with_each(x, axis, split_dim, concat_dim):
+    size, index = (lax.axis_size(axis), lax.axis_index(axis))
+    blocks = in_blocks(x, split_dim, size)
+    outs = [blocks[index]]
+    for step in range(1, size):
+        sent = blocks[index ^ step]
+        outs.append(lax.ppermute(sent, axis, [(i, i ^ step) for i in range(size)]))
+    blocks = jnp.stack(outs)[index ^ jnp.arange(size)]
+    return in_order(blocks, concat_dim)
 
 
 def rms_scale(values, gain_row):
@@ -131,7 +154,7 @@
     received = attend_grouped(
         (
             lax.all_to_all(query_split, "space", split_axis=1, concat_axis=0, tiled=True),
-            lax.all_to_all(key_split, "space", split_axis=1, concat_axis=0, tiled=True),
+            swapped_with_each(key_split, "space", 1, 0),
             lax.all_to_all(value_split, "space", split_axis=1, concat_axis=0, tiled=True),
         ),
         block_lists=block_lists,

time: 111 us -> 102 us (0.919)
  waiting for transfers between devices: 27.9 us -> 21.4 us
  local copies, waits for them, and re-layouts: 22.8 us -> 21.6 us
    all_to_all x1 -> x0, waiting for transfers between devices: 7.49 us -> none  [body(): lax.all_to_all(key_split, 'space', split_axis=1, concat_axis=0, tiled=True)]
    all_to_all x1 -> x0, starting transfers between devices: 4.24 us -> none  [body(): lax.all_to_all(key_split, 'space', split_axis=1, concat_axis=0, tiled=True)]
    ppermute x0 -> x3, starting transfers between devices: none -> 3.28 us  [swapped_with_each(): outs.append(lax.ppermute(sent, axis, [(i, i ^ step) for i in range(size)]))]
    select_n x1, other arithmetic: 2.84 us -> 0.21 us  [attend_group(): jnp.take(key_blocks, chosen, axis=0)]
    select_n x1 -> x2, other arithmetic: 0.01 us -> 2.17 us  [attend_group(): jnp.take(value_blocks, chosen, axis=0)]
    unnamed x31 -> x34, local copies, waits for them, and re-layouts: 7.03 us -> 5.85 us
  transfers between devices with their start and end apart: 4 -> 6, of which waited for: 4 -> 3; matrix products, arithmetic and copies ran while one was open for 11% -> 12% of each run, Pallas kernels for 0% -> 0%
where the time goes in v1:
time: 102 us; the launch traced here: 101 us
  blocking collectives  29.1 us (29%)
  local copies, waits for them, and re-layouts  21.6 us (21%)
  waiting for transfers between devices  21.4 us (21%)
  starting transfers between devices  16.5 us (16%)
  other arithmetic  7.54 us (7%)
  matrix products  4.28 us (4%)
    all_to_all x1, blocking collectives, body(): lax.all_to_all(mixed_tokens, 'tm', split_axis=0, concat_axis=1, tiled=True)  17.9 us
    all_to_all x1, waiting for transfers between devices, body(): lax.all_to_all(normed, 'tm', split_axis=1, concat_axis=0, tiled=True)  14.1 us
    all_to_all x1, blocking collectives, body(): lax.all_to_all(gathered, 'space', split_axis=0, concat_axis=1, tiled=True)  11.2 us
    all_to_all x1, starting transfers between devices, body(): lax.all_to_all(normed, 'tm', split_axis=1, concat_axis=0, tiled=True)  6.29 us
    unnamed x34, local copies, waits for them, and re-layouts  5.85 us
    all_to_all x1, waiting for transfers between devices, body(): lax.all_to_all(value_split, 'space', split_axis=1, concat_axis=0, tiled=T...  5.73 us
    unnamed x1, other arithmetic  3.74 us
    all_to_all x1, starting transfers between devices, body(): lax.all_to_all(value_split, 'space', split_axis=1, concat_axis=0, tiled=T...  3.47 us
  transfers between devices with their start and end apart: 6, of which 3 were waited for; matrix products, arithmetic and copies ran while one was open for 12% of the time, Pallas kernels for 0%

profile of v1, /device:TPU:0, one launch (start us, length us, event | category | flops | bytes accessed | tf_op | source)
XLA Modules:
  0.0 100.9 jit_solution(14381656075192199757)
XLA Ops:
  0.0 1.5 %reshape_reshape_reshape.9 = bf16[128,4,1,4,128]{4,3,1,0,2:T(4,128)(2,1)S(1)} reshape(bf16[1,128,2048]{2,1,0:T(8,128)(2,1)} %param.14) | data formatting | bytes 1048576 | tf_op jit(solution)/shard_map/reshape;reshape;reshape | solution.py:14
  1.5 0.2 constant_dynamic-slice_fusion.3
  1.7 3.0 %collective-permute-start.1 = (bf16[128,1,4,128]{3,0,2,1:T(8,128)(2,1)S(1)}, bf16[128,1,4,128]{3,0,2,1:T(8,128)(2,1)S(1)}, u32[]{:S(2)}, u32[]{:S(2)}) collective-permute-start(bf16[128,1,4,128]{3,0,2,1:T(8,128)(2,1)S(1)} %bitcast.123), channel_id=1, source_target_pairs={{0,2},{1,3},{2,0},{3,1},{4,6},{5,7},{6,4},{7,5},{8,10},{9,11},{10,... | collective-permute-start | bytes 393224 | tf_op jit(solution)/shard_map/ppermute | solution.py:30
  4.9 0.2 collective-permute-start
  5.1 0.3 copy.135
  5.4 1.1 %copy.136 = bf16[128,4,4,128]{3,2,0,1:T(4,128)(2,1)} copy(bf16[128,4,4,128]{0,3,2,1:T(8,128)(2,1)S(1)} %bitcast.117) | data formatting | bytes 1048576 | tf_op jit(solution)/shard_map/reshape;reshape | solution.py:153
  6.4 3.5 %all-to-all-start = ((bf16[128,4,4,128]{3,2,0,1:T(4,128)(2,1)}), bf16[128,4,4,128]{3,2,0,1:T(4,128)(2,1)S(1)}, u32[]{:S(2)}, u32[]{:S(2)}) async-start(bf16[128,4,4,128]{3,2,0,1:T(4,128)(2,1)} %copy.136), calls=%async_computation | async-start | bytes 1048576 | tf_op jit(solution)/shard_map/all_to_all | solution.py:158
  10.1 0.3 copy.143
  10.4 1.0 copy.144
  11.5 0.6 gather_fusion
  12.2 0.8 gather_fusion.2
  13.0 5.7 %all-to-all-done = bf16[128,4,4,128]{3,2,0,1:T(4,128)(2,1)S(1)} async-done(((bf16[128,4,4,128]{3,2,0,1:T(4,128)(2,1)}), bf16[128,4,4,128]{3,2,0,1:T(4,128)(2,1)S(1)}, u32[]{:S(2)}, u32[]{:S(2)}) %all-to-all-start) | async-done | bytes 524320 | tf_op jit(solution)/shard_map/all_to_all | solution.py:158
  18.7 3.5 %all-to-all-start.1 = ((bf16[128,4,4,128]{3,0,2,1:T(8,128)(2,1)}), bf16[128,4,4,128]{3,0,2,1:T(8,128)(2,1)S(1)}, u32[]{:S(2)}, u32[]{:S(2)}) async-start(bf16[128,4,4,128]{3,0,2,1:T(8,128)(2,1)} %copy.144), calls=%async_computation.1 | async-start | bytes 1048576 | tf_op jit(solution)/shard_map/all_to_all | solution.py:156
  22.2 0.2 broadcast_select_fusion
  22.4 0.2 copy.142
  22.6 3.2 %gather_fusion.1 = bf16[12,128,4,128]{3,2,1,0:T(4,128)(2,1)} fusion(bf16[4,128,4,128]{3,2,1,0:T(4,128)(2,1)S(1)} %bitcast.105, s32[1024]{0:T(1024)S(1)} %pad_clamp_fusion.1), kind=kCustom, calls=%fused_computation.clone | custom fusion | bytes 3145776 | tf_op jit(solution)/shard_map/while/body/eval_jaxpr/jit(_take)/gather | solution.py:57
  25.8 2.2 %broadcast_select_fusion.1 = bf16[4,3,128,4,128]{4,3,2,1,0:T(4,128)(2,1)S(1)} fusion(bf16[4,3,128,4,128]{4,3,2,1,0:T(4,128)(2,1)} %bitcast.108, pred[4,3]{1,0:T(4,128)(4,1)S(1)} %compare_and_fusion), kind=kLoop, calls=%fused_computation.12 | loop fusion | flops 786432 | bytes 3145740 | tf_op jit(solution)/shard_map/while/body/eval_jaxpr/jit(_take)/select_n | solution.py:57
  27.9 1.5 %copy.137 = bf16[4,3,128,4,128]{4,2,1,3,0:T(8,128)(2,1)} copy(bf16[4,3,128,4,128]{4,3,2,1,0:T(4,128)(2,1)S(1)} %broadcast_select_fusion.1) | data formatting | bytes 3145728 | tf_op jit(solution)/shard_map/while/body/eval_jaxpr/jit(_take)/select_n | solution.py:57
  29.5 1.5 %all-to-all-done.1 = bf16[128,4,4,128]{3,0,2,1:T(8,128)(2,1)S(1)} async-done(((bf16[128,4,4,128]{3,0,2,1:T(8,128)(2,1)}), bf16[128,4,4,128]{3,0,2,1:T(8,128)(2,1)S(1)}, u32[]{:S(2)}, u32[]{:S(2)}) %all-to-all-start.1) | async-done | bytes 524320 | tf_op jit(solution)/shard_map/all_to_all | solution.py:156
  31.0 0.6 bitcast_reduce_fusion
  31.6 0.5 fusion.1
  32.2 0.9 copy-done.1
  33.0 1.0 fusion.18
  34.1 0.4 copy.147
  34.5 11.2 %all_to_all.60 = bf16[512,4,128]{2,1,0:T(4,128)(2,1)S(1)} all-to-all(bf16[512,4,128]{2,1,0:T(4,128)(2,1)S(1)} %copy.147), channel_id=1, replica_groups=mesh['tm'=8,'space'=4] {'space'}, dimensions={0} | all-to-all | bytes 1048576 | tf_op jit(solution)/shard_map/all_to_all | solution.py:163
  45.8 0.3 copy.149
  46.1 0.2 multiply_reduce_fusion.1
  46.5 0.3 multiply_convert_fusion.1
  46.8 0.9 copy.150
  47.8 0.5 broadcast.189
  48.3 3.7 %reduce.7 = bf16[128,2048]{1,0:T(8,128)(2,1)S(1)} reduce(bf16[128,1,2048]{2,1,0:T(2,128)(2,1)S(1)} %bitcast.112, bf16[]{:T(256)} %broadcast.189), dimensions={1}, to_apply=%bitcast.90.reduce_sub_computation | reduce | bytes 1048578
  52.0 1.2 %reshape.260 = bf16[8,2,16384]{2,1,0:T(2,128)(2,1)} reshape(bf16[128,2048]{1,0:T(8,128)(2,1)S(1)} %reduce.7) | data formatting | bytes 1048576
  53.2 6.3 %all-to-all-start.3 = ((bf16[8,2,16384]{2,1,0:T(2,128)(2,1)}), bf16[8,2,16384]{2,1,0:T(2,128)(2,1)S(1)}, u32[]{:S(2)}, u32[]{:S(2)}) async-start(bf16[8,2,16384]{2,1,0:T(2,128)(2,1)} %reshape.260), calls=%async_computation.3 | async-start | bytes 1048576 | tf_op jit(solution)/shard_map/all_to_all | solution.py:167
  59.6 14.1 %all-to-all-done.3 = bf16[8,2,16384]{2,1,0:T(2,128)(2,1)S(1)} async-done(((bf16[8,2,16384]{2,1,0:T(2,128)(2,1)}), bf16[8,2,16384]{2,1,0:T(2,128)(2,1)S(1)}, u32[]{:S(2)}, u32[]{:S(2)}) %all-to-all-start.3) | async-done | bytes 524320 | tf_op jit(solution)/shard_map/all_to_all | solution.py:167
  73.7 0.5 reshape.261
  74.2 3.0 %bitcast_reduce_fusion.2 = bf16[128,2048]{1,0:T(8,128)(2,1)S(1)} fusion(bf16[128,1,2048]{2,1,0:T(2,128)(2,1)S(1)} %reshape.261), kind=kLoop, calls=%fused_computation.65 | loop fusion | bytes 1048576 | tf_op jit(solution)/shard_map/all_to_all | solution.py:167
  77.2 0.3 copy.164
  77.5 0.3 fusion.24
  77.8 0.3 copy-done.4
  78.2 0.3 fusion.26
  78.5 0.3 fusion.29
  78.7 0.4 fusion.14
  79.2 0.4 copy.156
  79.7 1.4 %multiply_reduce_fusion = (f32[8,16]{0,1:T(8,128)S(1)}, f32[8,16,16,128]{3,0,2,1:T(8,128)S(1)}) fusion(bf16[8,16,16,128]{3,2,1,0:T(8,128)(2,1)S(1)} %bitcast.119, f32[16]{0:T(128)S(1)} %copy-done.10, f32[16,8,8,16]{2,1,3,0:T(8,128)S(1)} %copy.156), kind=kOutput, calls=%fused_computation.24 | convolution fusion | flops 26476416 | bytes 1638976 | tf_op jit(solution)/shard_map/ktsh,skhp->tkhp/dot_general | solution.py:122
  81.2 0.2 copy.158
  81.6 0.4 copy-done.7
  82.2 17.9 %all_to_all.61 = bf16[8,16,2048]{2,1,0:T(8,128)(2,1)S(1)} all-to-all(bf16[8,16,2048]{2,1,0:T(8,128)(2,1)S(1)} %multiply_convert_fusion), channel_id=1, replica_groups=mesh['tm'=8,'space'=4] {'tm'}, dimensions={0} | all-to-all | bytes 1048576 | tf_op jit(solution)/shard_map/all_to_all | solution.py:171
  100.1 0.8 copy.192
  (46 shorter events, 1.2 us)
Async XLA Ops:
  0.0 77.5 %copy-start = (bf16[2048,64]{0,1:T(8,128)(2,1)S(1)}, bf16[2048,64]{0,1:T(8,128)(2,1)}, u32[]{:S(2)}) copy-start(bf16[2048,64]{0,1:T(8,128)(2,1)} %param.21) | copy-start | bytes 786436
  0.0 5.1 %copy-start.2 = (bf16[1,128,2048]{2,1,0:T(8,128)(2,1)S(1)}, bf16[1,128,2048]{2,1,0:T(8,128)(2,1)}, u32[]{:S(2)}) copy-start(bf16[1,128,2048]{2,1,0:T(8,128)(2,1)} %param.15) | copy-start | bytes 1572868
  1.7 9.7 %collective-permute-start.1 = (bf16[128,1,4,128]{3,0,2,1:T(8,128)(2,1)S(1)}, bf16[128,1,4,128]{3,0,2,1:T(8,128)(2,1)S(1)}, u32[]{:S(2)}, u32[]{:S(2)}) collective-permute-start(bf16[128,1,4,128]{3,0,2,1:T(8,128)(2,1)S(1)} %bitcast.123), channel_id=1, source_target_pairs={{0,2},{1,3},{2,0},{3,1},{4,6},{5,7},{6,4},{7,5},{8,10},{9,11},{10,... | collective-permute-start | bytes 393224 | tf_op jit(solution)/shard_map/ppermute | solution.py:30
  4.8 6.6 %collective-permute-start.2 = (bf16[128,1,4,128]{3,0,2,1:T(8,128)(2,1)S(1)}, bf16[128,1,4,128]{3,0,2,1:T(8,128)(2,1)S(1)}, u32[]{:S(2)}, u32[]{:S(2)}) collective-permute-start(bf16[128,1,4,128]{3,0,2,1:T(8,128)(2,1)S(1)} %bitcast.124), channel_id=1, source_target_pairs={{0,3},{1,2},{2,1},{3,0},{4,7},{5,6},{6,5},{7,4},{8,11},{9,10},{10,... | collective-permute-start | bytes 393224 | tf_op jit(solution)/shard_map/ppermute | solution.py:30
  4.9 5.0 %copy-start.8 = (s32[4,3]{1,0:T(4,128)S(1)}, s32[4,3]{1,0:T(4,128)}, u32[]{:S(2)}) copy-start(s32[4,3]{1,0:T(4,128)} %param.16) | copy-start | bytes 148
  4.9 5.2 %copy-start.3 = (bf16[1,128,2048]{2,1,0:T(8,128)(2,1)S(1)}, bf16[1,128,2048]{2,1,0:T(8,128)(2,1)}, u32[]{:S(2)}) copy-start(bf16[1,128,2048]{2,1,0:T(8,128)(2,1)} %param.13) | copy-start | bytes 1572868
  4.9 6.5 %collective-permute-start = (bf16[128,1,4,128]{3,0,2,1:T(8,128)(2,1)S(1)}, bf16[128,1,4,128]{3,0,2,1:T(8,128)(2,1)S(1)}, u32[]{:S(2)}, u32[]{:S(2)}) collective-permute-start(bf16[128,1,4,128]{3,0,2,1:T(8,128)(2,1)S(1)} %bitcast.125), channel_id=1, source_target_pairs={{0,1},{1,0},{2,3},{3,2},{4,5},{5,4},{6,7},{7,6},{8,9},{9,8},{10,11... | collective-permute-start | bytes 393224 | tf_op jit(solution)/shard_map/ppermute | solution.py:30
  6.4 12.3 %all-to-all-start = ((bf16[128,4,4,128]{3,2,0,1:T(4,128)(2,1)}), bf16[128,4,4,128]{3,2,0,1:T(4,128)(2,1)S(1)}, u32[]{:S(2)}, u32[]{:S(2)}) async-start(bf16[128,4,4,128]{3,2,0,1:T(4,128)(2,1)} %copy.136), calls=%async_computation | async-start | bytes 1048576 | tf_op jit(solution)/shard_map/all_to_all | solution.py:158
  18.7 12.3 %all-to-all-start.1 = ((bf16[128,4,4,128]{3,0,2,1:T(8,128)(2,1)}), bf16[128,4,4,128]{3,0,2,1:T(8,128)(2,1)S(1)}, u32[]{:S(2)}, u32[]{:S(2)}) async-start(bf16[128,4,4,128]{3,0,2,1:T(8,128)(2,1)} %copy.144), calls=%async_computation.1 | async-start | bytes 1048576 | tf_op jit(solution)/shard_map/all_to_all | solution.py:156
  31.6 1.4 %copy-start.1 = (bf16[4,3,128,4,128]{4,2,1,3,0:T(8,128)(2,1)S(1)}, bf16[4,3,128,4,128]{4,2,1,3,0:T(8,128)(2,1)}, u32[]{:S(2)}) copy-start(bf16[4,3,128,4,128]{4,2,1,3,0:T(8,128)(2,1)} %copy.137) | copy-start | bytes 4718596
  45.8 0.7 copy-start.6
  48.3 11.2 %copy-start.5 = (f32[8,16,16]{2,1,0:T(8,128)S(1)}, f32[8,16,16]{2,1,0:T(8,128)}, u32[]{:S(2)}) copy-start(f32[8,16,16]{2,1,0:T(8,128)} %param.17) | copy-start | bytes 24580
  48.3 11.3 %copy-start.9 = (f32[16]{0:T(128)S(1)}, f32[16]{0:T(128)}, u32[]{:S(2)}) copy-start(f32[16]{0:T(128)} %param.18) | copy-start | bytes 196
  53.2 20.5 %all-to-all-start.3 = ((bf16[8,2,16384]{2,1,0:T(2,128)(2,1)}), bf16[8,2,16384]{2,1,0:T(2,128)(2,1)S(1)}, u32[]{:S(2)}, u32[]{:S(2)}) async-start(bf16[8,2,16384]{2,1,0:T(2,128)(2,1)} %reshape.260), calls=%async_computation.3 | async-start | bytes 1048576 | tf_op jit(solution)/shard_map/all_to_all | solution.py:167
  77.2 1.0 copy-start.4
  78.7 1.0 copy-start.10
  81.4 0.7 copy-start.7
